TPU v7x, 32 devices: a whole 2x2x4 slice. The times are simulated.
32 devices in a mesh: expert: 8 (over y, x, core), dp: 4 (over z).
Axes of the slice: x: 2, y: 2, z: 4, core: 2. Of those that a mesh axis runs over, the one named last changes fastest.
Arguments:
- tokens: bfloat16 [4096, 2048], P(('expert', 'dp')), may hold values from -6 to 6
- out_grad: bfloat16 [4096, 2048], P(('expert', 'dp')), may hold values from -1.25 to 1.25
- expert_ids: int32 [4096, 8], P(('expert', 'dp')), may hold values from 0 to 15, all different within a row; in each aligned block of 128 rows (0 to 127, 128 to 255, ...) at most 72 rows name the same one
- route_weight: bfloat16 [4096, 8], P(('expert', 'dp')), may hold values from 0.099609375 to 1
- w_gate_up: bfloat16 [16, 2048, 768], P('expert'), may hold values from -0.125 to 0.125
- w_down: bfloat16 [16, 384, 2048], P('expert'), may hold values from -0.3125 to 0.3125
Outputs:
- d_tokens: bfloat16 [4096, 2048], P(('expert', 'dp'))
- d_route: bfloat16 [4096, 8], P(('expert', 'dp'))
- grad_gate_up: bfloat16 [16, 2048, 768], P('expert', 'dp')
- grad_down: bfloat16 [16, 384, 2048], P('expert', None, 'dp')
Inputs may be any that keep to these rules, and one draw needn't show every extreme that they name: `expert_ids`: each row names 8 different experts. Among the 128 rows of one device (aligned blocks of 128 rows) no expert is named more than 72 times, and in every draw some expert is named exactly 72 times by the rows of some device.
All inputs are finite; a program needn't handle non-finite values.
Results may differ from a plain program's by a relative error of at most 0.012.
Values may be sent and summed in bfloat16 or wider, within the bound.
A program may use at most 128 MiB of HBM per device.

v0:
```python
import jax
import jax.numpy as jnp
from jax import lax
from jax.sharding import PartitionSpec as P


def expert_backward(rows_in, rows_grad, weight, gate_up, down):
    pre_act = jnp.dot(rows_in, gate_up, preferred_element_type=jnp.float32)
    half_width = pre_act.shape[1] // 2
    gate_pre = pre_act[:, :half_width]
    up_pre = pre_act[:, half_width:]
    sigmoid_gate = jax.nn.sigmoid(gate_pre)
    active = gate_pre * sigmoid_gate
    hidden = (active * up_pre).astype(jnp.bfloat16)
    back_hidden = lax.dot_general(
        rows_grad, down, (((1,), (1,)), ((), ())), preferred_element_type=jnp.float32
    )
    route_grad = jnp.sum(back_hidden * hidden.astype(jnp.float32), axis=1).astype(jnp.bfloat16)
    weight_col = weight.astype(jnp.float32)[:, None]
    scaled = weight_col * back_hidden
    grad_gate = scaled * up_pre * sigmoid_gate * (1.0 + gate_pre * (1.0 - sigmoid_gate))
    grad_up = scaled * active
    grad_pre = jnp.concatenate([grad_gate, grad_up], axis=1).astype(jnp.bfloat16)
    route_input = lax.dot_general(
        grad_pre, gate_up, (((1,), (1,)), ((), ())), preferred_element_type=jnp.float32
    ).astype(jnp.bfloat16)
    scaled_hidden = (weight_col * hidden.astype(jnp.float32)).astype(jnp.bfloat16)
    return (route_input, route_grad, grad_pre, scaled_hidden)


def weight_terms(rows_in, rows_grad, grad_pre, scaled_hidden):
    term_gate_up = lax.dot_general(
        rows_in, grad_pre, (((0,), (0,)), ((), ())), preferred_element_type=jnp.float32
    )
    term_down = lax.dot_general(
        scaled_hidden, rows_grad, (((0,), (0,)), ((), ())), preferred_element_type=jnp.float32
    )
    return (term_gate_up, term_down)


def run_expert(arrived_in, arrived_grad, arrived_weight, gate_up, down):
    groups = arrived_in.shape[0]
    capacity = arrived_in.shape[1]
    dim_model = arrived_in.shape[2]
    rows_in = arrived_in.reshape(groups * capacity, dim_model)
    rows_grad = arrived_grad.reshape(groups * capacity, dim_model)
    weight = arrived_weight.reshape(groups * capacity)
    route_input, route_grad, grad_pre, scaled_hidden = expert_backward(
        rows_in, rows_grad, weight, gate_up, down
    )
    shaped_input = route_input.reshape(groups, capacity, dim_model)
    shaped_grad = route_grad.reshape(groups, capacity)
    return (shaped_input, shaped_grad, (rows_in, rows_grad, grad_pre, scaled_hidden))


def slot_numbers(route_experts, all_experts):
    route_count = route_experts.shape[0]
    block_len = 128
    block_count = route_count // block_len
    onehot = (route_experts[:, None] == jnp.arange(all_experts, dtype=jnp.int32)[None, :]).astype(
        jnp.bfloat16
    )
    onehot = onehot.reshape(block_count, block_len, all_experts)
    lower = (jnp.arange(block_len)[:, None] > jnp.arange(block_len)[None, :]).astype(jnp.bfloat16)
    within = jnp.einsum("ij,bje->bie", lower, onehot, preferred_element_type=jnp.float32)
    totals = jnp.sum(onehot.astype(jnp.float32), axis=1)
    earlier = (jnp.arange(block_count)[:, None] > jnp.arange(block_count)[None, :]).astype(
        jnp.float32
    )
    before = jnp.dot(earlier, totals, precision=lax.Precision.HIGHEST)
    counted = jnp.sum((within + before[:, None, :]) * onehot.astype(jnp.float32), axis=2)
    return counted.reshape(route_count).astype(jnp.int32)


def local(tokens, out_grad, expert_ids, route_weight, w_gate_up, w_down):
    tok_rows = tokens.shape[0]
    dim_model = tokens.shape[1]
    top_count = expert_ids.shape[1]
    exp_local = w_gate_up.shape[0]
    groups = lax.axis_size("expert")
    all_experts = exp_local * groups
    route_count = tok_rows * top_count
    capacity = 9 * tok_rows * top_count // (8 * all_experts)
    route_experts = expert_ids.reshape(route_count)
    slot_index = slot_numbers(route_experts, all_experts)
    target = route_experts // exp_local
    local_expert = route_experts % exp_local
    position = local_expert * (groups * capacity) + target * capacity + slot_index
    source_table = jnp.full((all_experts * capacity,), route_count, jnp.int32)
    source_table = source_table.at[position].set(jnp.arange(route_count, dtype=jnp.int32))
    token_of = source_table // top_count
    send_in = jnp.take(tokens, token_of, axis=0, mode="fill", fill_value=0).reshape(
        exp_local, groups, capacity, dim_model
    )
    send_grad = jnp.take(out_grad, token_of, axis=0, mode="fill", fill_value=0).reshape(
        exp_local, groups, capacity, dim_model
    )
    send_weight = jnp.take(
        route_weight.reshape(route_count), source_table, axis=0, mode="fill", fill_value=0
    ).reshape(exp_local, groups, capacity)
    gate_up_terms = []
    down_terms = []
    arrived_in, arrived_grad, arrived_weight = (
        lax.all_to_all(send_in, "expert", split_axis=1, concat_axis=1, tiled=True),
        lax.all_to_all(send_grad, "expert", split_axis=1, concat_axis=1, tiled=True),
        lax.all_to_all(send_weight, "expert", split_axis=1, concat_axis=1, tiled=True),
    )
    inputs_list = []
    grads_list = []
    saved = []
    for which in range(exp_local):
        shaped_input, shaped_grad, kept = run_expert(
            arrived_in[which],
            arrived_grad[which],
            arrived_weight[which],
            w_gate_up[which],
            w_down[which],
        )
        inputs_list.append(shaped_input)
        grads_list.append(shaped_grad)
        saved.append(kept)
    returned_in, returned_route = (
        lax.all_to_all(jnp.stack(inputs_list), "expert", split_axis=1, concat_axis=1, tiled=True),
        lax.all_to_all(jnp.stack(grads_list), "expert", split_axis=1, concat_axis=1, tiled=True),
    )
    for which in range(exp_local):
        term_gate_up, term_down = weight_terms(*saved[which])
        gate_up_terms.append(term_gate_up)
        down_terms.append(term_down)
    summed_gate_up, summed_down = (
        lax.psum_scatter(
            jnp.stack(gate_up_terms).astype(jnp.bfloat16), "dp", scatter_dimension=1, tiled=True
        ).astype(jnp.float32),
        lax.psum_scatter(
            jnp.stack(down_terms).astype(jnp.bfloat16), "dp", scatter_dimension=2, tiled=True
        ).astype(jnp.float32),
    )
    mean_factor = 1.0 / lax.axis_size("dp")
    grad_gate_up = (summed_gate_up * mean_factor).astype(jnp.bfloat16)
    grad_down = (summed_down * mean_factor).astype(jnp.bfloat16)
    back_flat = returned_in.reshape(all_experts * capacity, dim_model)
    route_flat = returned_route.reshape(all_experts * capacity)
    route_rows = jnp.take(back_flat, position, axis=0).reshape(tok_rows, top_count, dim_model)
    d_tokens = jnp.sum(route_rows.astype(jnp.float32), axis=1).astype(jnp.bfloat16)
    d_route = jnp.take(route_flat, position, axis=0).reshape(tok_rows, top_count)
    return (d_tokens, d_route, grad_gate_up, grad_down)


def solution(mesh):
    placed = (
        P(("expert", "dp"), None),
        P(("expert", "dp"), None),
        P(("expert", "dp"), None),
        P(("expert", "dp"), None),
        P("expert", None, None),
        P("expert", None, None),
    )
    return jax.shard_map(
        local,
        mesh=mesh,
        in_specs=placed,
        out_specs=(
            P(("expert", "dp"), None),
            P(("expert", "dp"), None),
            P("expert", "dp", None),
            P("expert", None, "dp"),
        ),
        check_vma=False,
    )
```

profile of v0, /device:TPU:1, one launch (start us, length us, event | category | flops | bytes accessed | tf_op | source)
XLA Modules:
  0.0 364.1 jit_solution(9369899892041569120)
XLA Ops:
  7.2 0.8 copy.32
  8.0 0.1 eq.19
  8.1 0.1 reshape.243
  8.2 0.1 convert_reduce_fusion
  8.3 0.1 fusion.63
  8.4 0.2 fusion.31
  8.7 4.3 %scatter_custom_fusion = s32[1152]{0:T(1024)S(1)} fusion(s32[1024]{0:T(1024)S(1)} %bitcast.83, s32[1024]{0:T(1024)S(1)} %iota.30, s32[]{:T(128)} %constant.102.clone.1), kind=kCustom, calls=%fused_computation.119 | custom fusion | bytes 4612 | tf_op jit(solution)/shard_map/scatter | solution.py:90
  13.0 0.8 copy.38
  13.8 0.1 reshape.244
  13.9 7.3 %gather_fusion = bf16[1152]{0:T(1024)(128)(2,1)S(1)} fusion(bf16[1024]{0:T(1024)(128)(2,1)S(1)} %reshape.244, s32[2048]{0:T(1024)S(1)} %pad_clamp_fusion.1), kind=kCustom, calls=%fused_computation.2 | custom fusion | bytes 9216 | tf_op jit(solution)/shard_map/jit(_take)/gather | solution.py:98
  21.2 0.1 select_n.99
  21.3 0.6 copy.39
  21.9 5.2 %all-to-all-start = ((bf16[2,8,72]{2,0,1:T(2,128)(2,1)}), bf16[2,8,72]{2,0,1:T(2,128)(2,1)S(1)}, u32[]{:S(2)}, u32[]{:S(2)}) async-start(bf16[2,8,72]{2,0,1:T(2,128)(2,1)} %copy.39), calls=%async_computation | async-start | bytes 8192 | tf_op jit(solution)/shard_map/all_to_all | solution.py:106
  27.2 5.9 %gather_fusion.3 = bf16[1152,2048]{1,0:T(8,128)(2,1)} fusion(bf16[128,2048]{1,0:T(8,128)(2,1)S(1)} %copy-done, s32[2048]{0:T(1024)S(1)} %pad_clamp_fusion), kind=kCustom, calls=%fused_computation.clone | custom fusion | bytes 9441792 | tf_op jit(solution)/shard_map/jit(_take)/gather | solution.py:95
  33.1 5.9 %gather_fusion.4 = bf16[1152,2048]{1,0:T(8,128)(2,1)} fusion(bf16[128,2048]{1,0:T(8,128)(2,1)S(1)} %copy-done.2, s32[2048]{0:T(1024)S(1)} %pad_clamp_fusion), kind=kCustom, calls=%fused_computation.1.clone | custom fusion | bytes 9441792 | tf_op jit(solution)/shard_map/jit(_take)/gather | solution.py:92
  39.0 5.7 %broadcast_select_fusion = (bf16[1152,2048]{1,0:T(8,128)(2,1)S(1)}, bf16[1152,2048]{1,0:T(8,128)(2,1)}) fusion(bf16[1152,2048]{1,0:T(8,128)(2,1)} %gather_fusion.4, pred[1152]{0:T(1024)(128)(4,1)S(1)} %get-tuple-element.25, bf16[1152,2048]{1,0:T(8,128)(2,1)} %gather_fusion.3), kind=kLoop, calls=%fused_computation.8 | loop fusion | flops 4718592 | bytes 18875520 | tf_op jit(solution)/shard_map/jit(_take)/select_n | solution.py:92
  44.8 2.6 copy.41
  47.3 4.6 %all-to-all-start.2 = ((bf16[2,8,72,2048]{3,2,0,1:T(8,128)(2,1)}), bf16[2,8,72,2048]{3,2,0,1:T(8,128)(2,1)}, u32[]{:S(2)}, u32[]{:S(2)}) async-start(bf16[2,8,72,2048]{3,2,0,1:T(8,128)(2,1)} %copy.41), calls=%async_computation.2 | async-start | bytes 9437184 | tf_op jit(solution)/shard_map/all_to_all | solution.py:104
  51.9 5.2 %copy.40 = bf16[2,8,72,2048]{3,2,0,1:T(8,128)(2,1)} copy(bf16[2,8,72,2048]{3,2,1,0:T(8,128)(2,1)} %bitcast.70) | data formatting | bytes 9437184 | tf_op jit(solution)/shard_map/reshape | solution.py:95
  57.1 46.0 %all-to-all-done.2 = bf16[2,8,72,2048]{3,2,0,1:T(8,128)(2,1)} async-done(((bf16[2,8,72,2048]{3,2,0,1:T(8,128)(2,1)}), bf16[2,8,72,2048]{3,2,0,1:T(8,128)(2,1)}, u32[]{:S(2)}, u32[]{:S(2)}) %all-to-all-start.2) | async-done | bytes 4718624 | tf_op jit(solution)/shard_map/all_to_all | solution.py:104
  103.1 8.0 %all-to-all-start.1 = ((bf16[2,8,72,2048]{3,2,0,1:T(8,128)(2,1)}), bf16[2,8,72,2048]{3,2,0,1:T(8,128)(2,1)}, u32[]{:S(2)}, u32[]{:S(2)}) async-start(bf16[2,8,72,2048]{3,2,0,1:T(8,128)(2,1)} %copy.40), calls=%async_computation.1 | async-start | bytes 9437184 | tf_op jit(solution)/shard_map/all_to_all | solution.py:105
  111.2 0.1 reshape.249
  111.3 0.1 reshape.250
  111.3 2.8 fusion.68
  114.1 1.4 copy-done.3
  115.5 5.2 %fusion.7 = f32[576,768]{1,0:T(8,128)} fusion(bf16[576,2048]{1,0:T(8,128)(2,1)S(1)} %bitcast.78, bf16[2,2048,768]{2,1,0:T(8,128)(2,1)} %param.12), kind=kOutput, calls=%fused_computation.21 | convolution fusion | flops 1811939328 | bytes 7274496 | tf_op jit(solution)/shard_map/dot_general | solution.py:8
  120.7 41.7 %all-to-all-done.1 = bf16[2,8,72,2048]{3,2,0,1:T(8,128)(2,1)} async-done(((bf16[2,8,72,2048]{3,2,0,1:T(8,128)(2,1)}), bf16[2,8,72,2048]{3,2,0,1:T(8,128)(2,1)}, u32[]{:S(2)}, u32[]{:S(2)}) %all-to-all-start.1) | async-done | bytes 4718624 | tf_op jit(solution)/shard_map/all_to_all | solution.py:105
  162.4 2.9 fusion.69
  165.3 0.4 copy-done.4
  165.7 0.5 copy-done.5
  166.2 2.5 fusion.32
  168.8 1.5 fusion.21
  170.3 2.0 fusion.3
  172.3 2.7 fusion.34
  175.0 1.5 fusion.22
  176.5 1.9 pad_maximum_fusion.2
  178.4 0.0 reduce-scatter.5.cloned.1.call-update
  178.5 0.3 reduce-scatter.3.cloned.1.call-start
  178.7 0.7 copy-done.6
  179.5 4.4 %fusion.15 = bf16[1,2048,768]{2,1,0:T(8,128)(2,1)S(1)} fusion(bf16[576,2048]{1,0:T(8,128)(2,1)} %bitcast.79, bf16[576,384]{1,0:T(8,128)(2,1)S(1)} %get-tuple-element.35, bf16[576,384]{1,0:T(8,128)(2,1)S(1)} %copy-done.6), kind=kOutput, calls=%fused_computation.26 | convolution fusion | flops 1815281664 | bytes 6389760 | tf_op jit(solution)/shard_map/dot_general | solution.py:32
  183.9 2.9 fusion.16
  186.9 3.2 pad_maximum_fusion
  190.0 0.0 reduce-scatter.3.cloned.1.call-update
  190.1 0.1 convert_element_type.134
  190.2 0.1 convert_element_type.138
  190.3 0.6 copy.45
  190.9 6.8 %all-to-all-start.4 = ((bf16[2,8,72]{2,0,1:T(2,128)(2,1)}), bf16[2,8,72]{2,0,1:T(2,128)(2,1)S(1)}, u32[]{:S(2)}, u32[]{:S(2)}) async-start(bf16[2,8,72]{2,0,1:T(2,128)(2,1)} %copy.45), calls=%async_computation.4 | async-start | bytes 8192 | tf_op jit(solution)/shard_map/all_to_all | solution.py:124
  197.7 4.3 %fusion.9 = bf16[576,2048]{1,0:T(8,128)(2,1)S(1)} fusion(bf16[2,2048,768]{2,1,0:T(8,128)(2,1)} %param.12, bf16[576,384]{1,0:T(8,128)(2,1)S(1)} %get-tuple-element.35, bf16[576,384]{1,0:T(8,128)(2,1)} %get-tuple-element.36), kind=kOutput, calls=%fused_computation.24 | convolution fusion | flops 1814888448 | bytes 6389760 | tf_op jit(solution)/shard_map/dot_general | solution.py:24
  202.0 2.0 fusion.12
  204.0 2.6 pad_maximum_fusion.1
  206.7 4.8 %all-to-all-start.3 = ((bf16[2,8,72,2048]{3,2,0,1:T(8,128)(2,1)}), bf16[2,8,72,2048]{3,2,0,1:T(8,128)(2,1)}, u32[]{:S(2)}, u32[]{:S(2)}) async-start(bf16[2,8,72,2048]{3,2,0,1:T(8,128)(2,1)} %pad_maximum_fusion.1), calls=%async_computation.3 | async-start | bytes 9437184 | tf_op jit(solution)/shard_map/all_to_all | solution.py:123
  211.5 0.1 convert_element_type.123
  211.6 0.1 reshape.248
  211.7 6.8 %gather_fusion.2 = bf16[1024]{0:T(1024)(128)(2,1)S(1)} fusion(bf16[1152]{0:T(1024)(128)(2,1)S(1)} %reshape.248, s32[1024]{0:T(1024)S(1)} %broadcast_clamp_fusion), kind=kCustom, calls=%fused_computation.4 | custom fusion | bytes 8192 | tf_op jit(solution)/shard_map/jit(_take)/gather | solution.py:145
  218.5 0.1 gather.23
  218.6 0.1 broadcast_select_fusion.2
  218.7 0.7 copy.47
  219.4 43.3 %all-to-all-done.3 = bf16[2,8,72,2048]{3,2,0,1:T(8,128)(2,1)} async-done(((bf16[2,8,72,2048]{3,2,0,1:T(8,128)(2,1)}), bf16[2,8,72,2048]{3,2,0,1:T(8,128)(2,1)}, u32[]{:S(2)}, u32[]{:S(2)}) %all-to-all-start.3) | async-done | bytes 4718624 | tf_op jit(solution)/shard_map/all_to_all | solution.py:123
  262.6 5.3 %copy.44 = bf16[2,8,72,2048]{3,2,1,0:T(8,128)(2,1)} copy(bf16[2,8,72,2048]{3,2,0,1:T(8,128)(2,1)} %all-to-all-done.3) | data formatting | bytes 9437184 | tf_op jit(solution)/shard_map/all_to_all | solution.py:123
  267.9 11.8 %gather_fusion.1 = bf16[1024,2048]{1,0:T(8,128)(2,1)} fusion(bf16[1152,2048]{1,0:T(8,128)(2,1)} %bitcast.69, s32[1024]{0:T(1024)S(1)} %broadcast_clamp_fusion), kind=kCustom, calls=%fused_computation.3 | custom fusion | bytes 8392704 | tf_op jit(solution)/shard_map/jit(_take)/gather | solution.py:143
  279.7 5.2 %fusion = bf16[128,2048]{1,0:T(8,128)(2,1)} fusion(bf16[1024,2048]{1,0:T(8,128)(2,1)} %gather_fusion.1, pred[128,8]{1,0:T(8,128)(4,1)S(1)} %get-tuple-element.20), kind=kLoop, calls=%fused_computation.11 | loop fusion | flops 3932160 | bytes 4719616 | tf_op jit(solution)/shard_map/reduce_sum | solution.py:144
  284.9 2.2 multiply_convert_fusion.1
  287.0 67.4 %reduce-scatter.3.cloned.1.call-done = bf16[2,512,768]{2,1,0:T(8,128)(2,1)} async-done(((bf16[2,2048,768]{2,1,0:T(8,128)(2,1)}), bf16[2,512,768]{2,1,0:T(8,128)(2,1)}) %reduce-scatter.3.cloned.1.call-update) | async-done | bytes 1572880 | tf_op jit(solution)/shard_map/reduce_scatter | solution.py:131
  354.4 2.8 multiply_convert_fusion
  (44 shorter events, 0.2 us)
Async XLA Ops:
  7.2 20.0 %copy-start = (bf16[128,2048]{1,0:T(8,128)(2,1)S(1)}, bf16[128,2048]{1,0:T(8,128)(2,1)}, u32[]{:S(2)}) copy-start(bf16[128,2048]{1,0:T(8,128)(2,1)} %param.9) | copy-start | bytes 1572868
  21.9 25.4 %all-to-all-start = ((bf16[2,8,72]{2,0,1:T(2,128)(2,1)}), bf16[2,8,72]{2,0,1:T(2,128)(2,1)S(1)}, u32[]{:S(2)}, u32[]{:S(2)}) async-start(bf16[2,8,72]{2,0,1:T(2,128)(2,1)} %copy.39), calls=%async_computation | async-start | bytes 8192 | tf_op jit(solution)/shard_map/all_to_all | solution.py:106
  27.2 5.9 %copy-start.2 = (bf16[128,2048]{1,0:T(8,128)(2,1)S(1)}, bf16[128,2048]{1,0:T(8,128)(2,1)}, u32[]{:S(2)}) copy-start(bf16[128,2048]{1,0:T(8,128)(2,1)} %param.8) | copy-start | bytes 1572868
  47.3 55.8 %all-to-all-start.2 = ((bf16[2,8,72,2048]{3,2,0,1:T(8,128)(2,1)}), bf16[2,8,72,2048]{3,2,0,1:T(8,128)(2,1)}, u32[]{:S(2)}, u32[]{:S(2)}) async-start(bf16[2,8,72,2048]{3,2,0,1:T(8,128)(2,1)} %copy.41), calls=%async_computation.2 | async-start | bytes 9437184 | tf_op jit(solution)/shard_map/all_to_all | solution.py:104
  103.1 59.3 %all-to-all-start.1 = ((bf16[2,8,72,2048]{3,2,0,1:T(8,128)(2,1)}), bf16[2,8,72,2048]{3,2,0,1:T(8,128)(2,1)}, u32[]{:S(2)}, u32[]{:S(2)}) async-start(bf16[2,8,72,2048]{3,2,0,1:T(8,128)(2,1)} %copy.40), calls=%async_computation.1 | async-start | bytes 9437184 | tf_op jit(solution)/shard_map/all_to_all | solution.py:105
  111.2 173.7 %reduce-scatter.5.cloned.1.call-start = ((), (), s32[]{:S(2)}) async-start(), calls=%async_computation.8 | async-start | bytes 3932160 | tf_op jit(solution)/shard_map/reduce_scatter | solution.py:134
  114.1 1.4 copy-start.3
  162.4 3.3 copy-start.4
  162.4 3.8 %copy-start.5 = (f32[576,768]{1,0:T(8,128)S(1)}, f32[576,768]{1,0:T(8,128)}, u32[]{:S(2)}) copy-start(f32[576,768]{1,0:T(8,128)} %fusion.7) | copy-start | bytes 5308420
  162.4 7.9 %slice-start = ((s8[6291456]{0:T(1024)(128)(4,1)}), s8[4194304]{0:T(1024)(128)(4,1)S(1)}, s32[]{:S(2)}) async-start(s8[6291456]{0:T(1024)(128)(4,1)} %bitcast.85), calls=%async_computation.9 | async-start | bytes 8388608
  166.2 4.0 %slice-start.1 = ((s8[6291456]{0:T(1024)(128)(4,1)}), s8[2097152]{0:T(1024)(128)(4,1)S(1)}, s32[]{:S(2)}) async-start(s8[6291456]{0:T(1024)(128)(4,1)} %bitcast.85), calls=%async_computation.10 | async-start | bytes 4194304
  178.4 1.0 copy-start.6
  178.5 175.9 %reduce-scatter.3.cloned.1.call-start = ((), (), s32[]{:S(2)}) async-start(), calls=%async_computation.7 | async-start | bytes 7864320 | tf_op jit(solution)/shard_map/reduce_scatter | solution.py:131
  179.5 4.4 %copy-start.7 = (bf16[576,384]{1,0:T(8,128)(2,1)S(1)}, bf16[576,384]{1,0:T(8,128)(2,1)}, u32[]{:S(2)}) copy-start(bf16[576,384]{1,0:T(8,128)(2,1)} %get-tuple-element.37) | copy-start | bytes 1327108
  179.5 4.4 %copy-start.9 = (bf16[576,384]{1,0:T(8,128)(2,1)S(1)}, bf16[576,384]{1,0:T(8,128)(2,1)}, u32[]{:S(2)}) copy-start(bf16[576,384]{1,0:T(8,128)(2,1)} %get-tuple-element.38) | copy-start | bytes 1327108
  190.0 11.9 %slice-start.2 = ((s8[6291456]{0:T(1024)(128)(4,1)}), s8[2097152]{0:T(1024)(128)(4,1)S(1)}, s32[]{:S(2)}) async-start(s8[6291456]{0:T(1024)(128)(4,1)} %bitcast.87), calls=%async_computation.11 | async-start | bytes 4194304
  190.9 15.8 %all-to-all-start.4 = ((bf16[2,8,72]{2,0,1:T(2,128)(2,1)}), bf16[2,8,72]{2,0,1:T(2,128)(2,1)S(1)}, u32[]{:S(2)}, u32[]{:S(2)}) async-start(bf16[2,8,72]{2,0,1:T(2,128)(2,1)} %copy.45), calls=%async_computation.4 | async-start | bytes 8192 | tf_op jit(solution)/shard_map/all_to_all | solution.py:124
  197.7 4.3 %slice-start.3 = ((s8[6291456]{0:T(1024)(128)(4,1)}), s8[4194304]{0:T(1024)(128)(4,1)S(1)}, s32[]{:S(2)}) async-start(s8[6291456]{0:T(1024)(128)(4,1)} %bitcast.87), calls=%async_computation.12 | async-start | bytes 8388608
  197.7 4.3 %copy-start.8 = (bf16[576,384]{1,0:T(8,128)(2,1)S(1)}, bf16[576,384]{1,0:T(8,128)(2,1)}, u32[]{:S(2)}) copy-start(bf16[576,384]{1,0:T(8,128)(2,1)} %get-tuple-element.37) | copy-start | bytes 1327108
  197.7 4.3 %copy-start.10 = (bf16[576,384]{1,0:T(8,128)(2,1)S(1)}, bf16[576,384]{1,0:T(8,128)(2,1)}, u32[]{:S(2)}) copy-start(bf16[576,384]{1,0:T(8,128)(2,1)} %get-tuple-element.38) | copy-start | bytes 1327108
  206.7 56.0 %all-to-all-start.3 = ((bf16[2,8,72,2048]{3,2,0,1:T(8,128)(2,1)}), bf16[2,8,72,2048]{3,2,0,1:T(8,128)(2,1)}, u32[]{:S(2)}, u32[]{:S(2)}) async-start(bf16[2,8,72,2048]{3,2,0,1:T(8,128)(2,1)} %pad_maximum_fusion.1), calls=%async_computation.3 | async-start | bytes 9437184 | tf_op jit(solution)/shard_map/all_to_all | solution.py:123
  279.7 77.5 %copy-start.1 = (bf16[128,2048]{1,0:T(8,128)(2,1)S(1)}, bf16[128,2048]{1,0:T(8,128)(2,1)}, u32[]{:S(2)}) copy-start(bf16[128,2048]{1,0:T(8,128)(2,1)} %param.9) | copy-start | bytes 1572868
Sparse Core Ops, SparseCore 0:
  178.6 62.4 reduce-scatter.4
  243.4 110.9 reduce-scatter.2
where the time goes:
time: 365 us; the launch traced here: 364 us
  waiting for transfers between devices  198 us (54%)
  local copies, waits for them, and re-layouts  68.2 us (19%)
  starting transfers between devices  29.7 us (8%)
  matrix products  29.4 us (8%)
  other arithmetic  24 us (7%)
  between operations  14.4 us (4%)
    reduce_scatter x1, waiting for transfers between devices, local(): lax.psum_scatter(jnp.stack(gate_up_terms).astype(jnp.bfloat16), 'dp', sca...  67.4 us
    all_to_all x1, waiting for transfers between devices, local(): lax.all_to_all(send_in, 'expert', split_axis=1, concat_axis=1, tiled=True)  46 us
    all_to_all x1, waiting for transfers between devices, local(): lax.all_to_all(jnp.stack(inputs_list), 'expert', split_axis=1, concat_axi...  43.3 us
    all_to_all x1, waiting for transfers between devices, local(): lax.all_to_all(send_grad, 'expert', split_axis=1, concat_axis=1, tiled=True)  41.7 us
    gather x1, local copies, waits for them, and re-layouts, local(): jnp.take(back_flat, position, axis=0)  11.8 us
    all_to_all x1, starting transfers between devices, local(): lax.all_to_all(send_grad, 'expert', split_axis=1, concat_axis=1, tiled=True)  8.03 us
    dot_general x2, matrix products, weight_terms(): lax.dot_general(rows_in, grad_pre, (((0,), (0,)), ((), ())), preferred_el...  7.36 us
  transfers between devices with their start and end apart: 7, of which 4 were waited for; matrix products, arithmetic and copies ran while one was open for 24% of the time, Pallas kernels for 0%

commit v1 on v0

--- a/solution.py
+++ b/solution.py
@@ -1,7 +1,272 @@
+import functools
 import jax
 import jax.numpy as jnp
 from jax import lax
+from jax.experimental import pallas as pl
+from jax.experimental.pallas import tpu as pltpu
 from jax.sharding import PartitionSpec as P
+
+MESH = pl.DeviceIdType.MESH
+PAD = 128
+
+
+def fused_kernel(tok, gaug, wgu, wd, t_all, g_all, o_gu, o_dn, o_tok,
+                 xbuf, gbuf, gp, sh, dr, acc_gu, acc_dn, part, half, last,
+                 rt, rg, st, sg, zt, zg, loc, pr, ps, fr, fs):
+    rows = tok.shape[0]
+    dm = tok.shape[1]
+    e = lax.axis_index("expert")
+    z = lax.axis_index("dp")
+    e_c = e + 1 - 2 * (e % 2)
+    e_x = e + 2 - 4 * ((e // 2) % 2)
+    e_y = e + 4 - 8 * ((e // 4) % 2)
+    e_xy = e_y + 2 - 4 * ((e // 2) % 2)
+    z_off = (z, z + 1 - 2 * (z % 2), z + 2 - 4 * (z // 2), 3 - z)
+
+    barrier = pltpu.get_barrier_semaphore()
+    for peer in ((e_c, z), (e_x, z), (e_y, z), (e_xy, z), (e, z_off[1]), (e, z_off[2]), (e, z_off[3])):
+        pl.semaphore_signal(barrier, inc=1, device_id=peer, device_id_type=MESH)
+    pl.semaphore_wait(barrier, 7)
+
+    def blk(buf, u, k):
+        return buf.at[u, pl.ds(k * rows, rows)]
+
+    def copy(buf, recv, send, kind, su, sk, du, dk, dev):
+        return pltpu.make_async_remote_copy(
+            src_ref=blk(buf, su, sk), dst_ref=blk(buf, du, dk),
+            send_sem=send.at[kind, su, sk], recv_sem=recv.at[du, dk],
+            device_id=(dev, z), device_id_type=MESH)
+
+    def t_x(u, k): return copy(t_all, rt, st, 0, u, k, u, k + 1, e_x)
+    def t_y(u, k): return copy(t_all, rt, st, 1, u, k, u, k + 2, e_y)
+    def t_c(u, k): return copy(t_all, rt, st, 2, u, k, u + 1, k, e_c)
+    def g_x(u, k): return copy(g_all, rg, sg, 0, u, k, u, k + 1, e_x)
+    def g_y(u, k): return copy(g_all, rg, sg, 1, u, k, u, k + 2, e_y)
+    def g_c(u, k): return copy(g_all, rg, sg, 2, u, k, u + 1, k, e_c)
+
+    def zcopy(buf, recv, send, dz):
+        return pltpu.make_async_remote_copy(
+            src_ref=blk(buf, 0, 0), dst_ref=blk(buf, 2 * dz, 0),
+            send_sem=send.at[dz - 1], recv_sem=recv.at[2 * dz, 0],
+            device_id=(e, z_off[dz]), device_id_type=MESH)
+
+    def got(buf, recv, u, k):
+        pltpu.make_async_remote_copy(
+            src_ref=blk(buf, u, k), dst_ref=blk(buf, u, k),
+            send_sem=zt.at[0], recv_sem=recv.at[u, k],
+            device_id=(e_c, z), device_id_type=MESH).wait_recv()
+
+    def issue(u):
+        t_x(u, 0).start()
+        g_y(u, 0).start()
+        t_y(u, 0).start()
+        g_x(u, 0).start()
+        t_c(u, 0).start()
+        g_c(u, 0).start()
+
+    a = pltpu.make_async_copy(tok, blk(t_all, 0, 0), loc.at[0])
+    b = pltpu.make_async_copy(gaug, blk(g_all, 0, 0), loc.at[1])
+    a.start()
+    b.start()
+    a.wait()
+    b.wait()
+    issue(0)
+    for dz in (1, 2, 3):
+        zcopy(t_all, rt, zt, dz).start()
+        zcopy(g_all, rg, zg, dz).start()
+    acc_gu[...] = jnp.zeros_like(acc_gu)
+    acc_dn[...] = jnp.zeros_like(acc_dn)
+
+    width_gu = acc_gu.shape[1]
+    width_dn = acc_dn.shape[2]
+    ff = wd.shape[1]
+    count = wgu.shape[0]
+
+    def unit(u):
+        ca = pltpu.make_async_copy(t_all.at[u], xbuf, loc.at[0])
+        cb = pltpu.make_async_copy(g_all.at[u], gbuf, loc.at[1])
+        ca.start()
+        cb.start()
+        ca.wait()
+        cb.wait()
+        dr[...] = jnp.zeros_like(dr)
+
+        @pl.loop(0, count)
+        def _(j):
+            lane = lax.broadcasted_iota(jnp.int32, (xbuf.shape[0], PAD), 1)
+            mine = lane == e * count + j
+            tail = gbuf[:, dm:].astype(jnp.float32)
+            wcol = jnp.sum(jnp.where(mine, tail, 0.0), axis=1, keepdims=True)
+            pre = jnp.dot(xbuf[...], wgu[j], preferred_element_type=jnp.float32)
+            back = lax.dot_general(gbuf[:, :dm], wd[j], (((1,), (1,)), ((), ())),
+                                   preferred_element_type=jnp.float32)
+            gate = pre[:, :ff]
+            up = pre[:, ff:]
+            sig = jax.nn.sigmoid(gate)
+            act = gate * sig
+            hid = (act * up).astype(jnp.bfloat16).astype(jnp.float32)
+            dr[...] += jnp.where(mine, jnp.sum(back * hid, axis=1, keepdims=True), 0.0)
+            sc = wcol * back
+            gp[j, :, :ff] = (sc * up * sig * (1.0 + gate * (1.0 - sig))).astype(jnp.bfloat16)
+            gp[j, :, ff:] = (sc * act).astype(jnp.bfloat16)
+            sh[...] = (wcol * hid).astype(jnp.bfloat16)
+            cols = pl.ds(pl.multiple_of(z * width_gu, 128), width_gu)
+            cold = pl.ds(pl.multiple_of(z * width_dn, 128), width_dn)
+            acc_gu[j] += lax.dot_general(xbuf[:, cols], gp[j], (((0,), (0,)), ((), ())),
+                                         preferred_element_type=jnp.float32)
+            acc_dn[j] += lax.dot_general(sh[...], gbuf[:, cold], (((0,), (0,)), ((), ())),
+                                         preferred_element_type=jnp.float32)
+
+    def partial(c):
+        step = 512
+
+        @pl.loop(0, dm // step)
+        def _(n):
+            cols = pl.ds(pl.multiple_of(n * step, 128), step)
+            total = lax.dot_general(gp[0], wgu[0, cols, :], (((1,), (1,)), ((), ())),
+                                    preferred_element_type=jnp.float32)
+            for j in range(1, count):
+                total += lax.dot_general(gp[j], wgu[j, cols, :], (((1,), (1,)), ((), ())),
+                                         preferred_element_type=jnp.float32)
+            part[c, :, cols] = total.astype(jnp.bfloat16)
+        part[c, :, dm:] = dr[...].astype(jnp.bfloat16)
+
+    to_core = pltpu.make_async_remote_copy(
+        src_ref=part.at[1], dst_ref=half, send_sem=ps, recv_sem=pr,
+        device_id=(e_c, z), device_id_type=MESH)
+    to_owner = [pltpu.make_async_remote_copy(
+        src_ref=part.at[0, pl.ds(k * rows, rows)], dst_ref=last.at[k - 1],
+        send_sem=fs.at[k - 1], recv_sem=fr.at[k - 1],
+        device_id=(dev, z), device_id_type=MESH) for k, dev in ((1, e_x), (2, e_y), (3, e_xy))]
+
+    @pl.loop(0, 5)
+    def _(i):
+        u = 2 * i
+
+        @pl.when(i > 0)
+        def _():
+            unit(2 * i - 1)
+
+        @pl.when(i == 1)
+        def _():
+            partial(1)
+            to_core.start()
+
+        @pl.when(i < 4)
+        def _():
+            got(t_all, rt, u, 1)
+            t_y(u, 1).start()
+            t_c(u, 1).start()
+            got(g_all, rg, u, 2)
+            g_x(u, 2).start()
+            g_c(u, 2).start()
+
+        @pl.when(i > 0)
+        def _():
+            unit(2 * i - 2)
+
+        @pl.when(i == 1)
+        def _():
+            partial(0)
+            to_core.wait_recv()
+            part[0] = (part[0].astype(jnp.float32) + half[...].astype(jnp.float32)).astype(jnp.bfloat16)
+            for c in to_owner:
+                c.start()
+
+        @pl.when(i < 4)
+        def _():
+            got(g_all, rg, u, 1)
+            g_c(u, 1).start()
+            got(t_all, rt, u, 2)
+            t_c(u, 2).start()
+
+        @pl.when(i < 3)
+        def _():
+            got(t_all, rt, u + 2, 0)
+            got(g_all, rg, u + 2, 0)
+            issue(u + 2)
+
+        @pl.when(i < 4)
+        def _():
+            got(t_all, rt, u, 3)
+            t_c(u, 3).start()
+            got(g_all, rg, u, 3)
+            g_c(u, 3).start()
+            for k in range(4):
+                got(t_all, rt, u + 1, k)
+                got(g_all, rg, u + 1, k)
+
+    o_gu[...] = (acc_gu[...] * (1.0 / lax.axis_size("dp"))).astype(jnp.bfloat16)
+    o_dn[...] = (acc_dn[...] * (1.0 / lax.axis_size("dp"))).astype(jnp.bfloat16)
+    for c in to_owner:
+        c.wait_recv()
+    total = part[0, pl.ds(0, rows), :].astype(jnp.float32)
+    for k in range(3):
+        total += last[k].astype(jnp.float32)
+    o_tok[...] = total.astype(jnp.bfloat16)
+
+    to_core.wait_send()
+    for c in to_owner:
+        c.wait_send()
+    for dz in (1, 2, 3):
+        zcopy(t_all, rt, zt, dz).wait_send()
+        zcopy(g_all, rg, zg, dz).wait_send()
+
+    @pl.loop(0, 4)
+    def _(i):
+        u = 2 * i
+        for c in (t_x(u, 0), t_y(u, 0), t_y(u, 1), g_x(u, 0), g_y(u, 0), g_x(u, 2)):
+            c.wait_send()
+        for k in range(4):
+            t_c(u, k).wait_send()
+            g_c(u, k).wait_send()
+
+
+def local_fused(tokens, out_grad, expert_ids, route_weight, w_gate_up, w_down):
+    rows, dm = tokens.shape
+    count, _, width = w_gate_up.shape
+    ff = w_down.shape[1]
+    n_dp = lax.axis_size("dp")
+    units = 2 * n_dp
+    lanes = jnp.arange(PAD, dtype=jnp.int32)
+    onehot = expert_ids[:, :, None] == lanes[None, None, :]
+    dense = jnp.sum(jnp.where(onehot, route_weight[:, :, None].astype(jnp.float32), 0.0), axis=1)
+    gaug = jnp.concatenate([out_grad, dense.astype(jnp.bfloat16)], axis=1)
+    bf, f32 = jnp.bfloat16, jnp.float32
+    dma = pltpu.SemaphoreType.DMA
+    vm = pl.BlockSpec(memory_space=pltpu.VMEM)
+    anyw = pl.BlockSpec(memory_space=pl.ANY)
+    _, _, o_gu, o_dn, o_tok = pl.pallas_call(
+        fused_kernel,
+        out_shape=(
+            jax.ShapeDtypeStruct((units, 4 * rows, dm), bf),
+            jax.ShapeDtypeStruct((units, 4 * rows, dm + PAD), bf),
+            jax.ShapeDtypeStruct((count, dm // n_dp, width), bf),
+            jax.ShapeDtypeStruct((count, ff, dm // n_dp), bf),
+            jax.ShapeDtypeStruct((rows, dm + PAD), bf),
+        ),
+        in_specs=[vm] * 4,
+        out_specs=(anyw, anyw, vm, vm, vm),
+        scratch_shapes=[
+            pltpu.VMEM((4 * rows, dm), bf),
+            pltpu.VMEM((4 * rows, dm + PAD), bf),
+            pltpu.VMEM((count, 4 * rows, width), bf),
+            pltpu.VMEM((4 * rows, ff), bf),
+            pltpu.VMEM((4 * rows, PAD), f32),
+            pltpu.VMEM((count, dm // n_dp, width), f32),
+            pltpu.VMEM((count, ff, dm // n_dp), f32),
+            pltpu.VMEM((2, 4 * rows, dm + PAD), bf),
+            pltpu.VMEM((4 * rows, dm + PAD), bf),
+            pltpu.VMEM((3, rows, dm + PAD), bf),
+            dma((units, 4)), dma((units, 4)), dma((3, units, 4)), dma((3, units, 4)),
+            dma((3,)), dma((3,)), dma((2,)),
+            dma, dma, dma((3,)), dma((3,)),
+        ],
+        compiler_params=pltpu.CompilerParams(
+            collective_id=0, has_side_effects=True, vmem_limit_bytes=60 * 1024 * 1024),
+    )(tokens, gaug, w_gate_up, w_down)
+    d_route = jnp.sum(jnp.where(onehot, o_tok[:, None, dm:].astype(f32), 0.0), axis=2).astype(bf)
+    return o_tok[:, :dm], d_route, o_gu, o_dn
 
 
 def expert_backward(rows_in, rows_grad, weight, gate_up, down):
@@ -155,8 +420,9 @@
         P("expert", None, None),
         P("expert", None, None),
     )
+    small = mesh.shape["expert"] == 8 and mesh.shape["dp"] == 4
     return jax.shard_map(
-        local,
+        local_fused if small else local,
         mesh=mesh,
         in_specs=placed,
         out_specs=(

time: 365 us -> 233 us (0.64)
  Pallas kernels: 0 us -> 221 us
  waiting for transfers between devices: 198 us -> 0 us
  local copies, waits for them, and re-layouts: 68.2 us -> 7.72 us
  starting transfers between devices: 29.7 us -> 0 us
  matrix products: 29.4 us -> 0 us
  other arithmetic: 24 us -> 3.41 us
  between operations: 14.4 us -> 0.65 us
    pallas_call x0 -> x1, Pallas kernels: none -> 221 us  [local_fused(): pl.pallas_call(fused_kernel, out_shape=(jax.ShapeDtypeStruct((units, 4 *...]
    all_to_all x5 -> x0, waiting for transfers between devices: 131 us -> none  [the longest x1 46 us: local(): lax.all_to_all(send_in, 'expert', split_axis=1, concat_axis=1, tiled=True)]
    reduce_scatter x2 -> x0, waiting for transfers between devices: 67.4 us -> none  [the longest x1 67.4 us: local(): lax.psum_scatter(jnp.stack(gate_up_terms).astype(jnp.bfloat16), 'dp', sca...]
    gather x6 -> x0, local copies, waits for them, and re-layouts: 37.8 us -> none  [the longest x1 11.8 us: local(): jnp.take(back_flat, position, axis=0)]
    all_to_all x5 -> x0, starting transfers between devices: 29.5 us -> none  [the longest x1 8.03 us: local(): lax.all_to_all(send_grad, 'expert', split_axis=1, concat_axis=1, tiled=True)]
    dot_general x12 -> x0, matrix products: 29.4 us -> none  [the longest x2 7.36 us: weight_terms(): lax.dot_general(rows_in, grad_pre, (((0,), (0,)), ((), ())), preferred_el...]
    reshape x5 -> x0, local copies, waits for them, and re-layouts: 8.04 us -> none  [the longest x1 5.18 us: local(): jnp.take(out_grad, token_of, axis=0, mode='fill', fill_value=0)]
    another operation x4 -> x0, other arithmetic: 7.75 us -> none  [the longest x1 3.18 us: local(): jnp.stack(gate_up_terms).astype(jnp.bfloat16)]
  transfers between devices with their start and end apart: 7 -> 0, of which waited for: 4 -> 0; matrix products, arithmetic and copies ran while one was open for 24% -> 0% of each run, Pallas kernels for 0% -> 0%
where the time goes in v1:
time: 233 us; the launch traced here: 232 us
  Pallas kernels  221 us (95%)
  local copies, waits for them, and re-layouts  7.72 us (3%)
  other arithmetic  3.41 us (1%)
    pallas_call x1, Pallas kernels, local_fused(): pl.pallas_call(fused_kernel, out_shape=(jax.ShapeDtypeStruct((units, 4 *...  221 us
    unnamed x6, local copies, waits for them, and re-layouts  5.05 us

profile of v1, /device:TPU:1, one launch (start us, length us, event | category | flops | bytes accessed | tf_op | source)
XLA Modules:
  0.0 232.4 jit_solution(16955071481518775633)
XLA Ops:
  0.6 0.8 copy.12
  1.4 0.8 copy.13
  2.2 0.4 select_reduce_fusion.1
  2.6 1.9 pad_maximum_fusion.gaug
  4.5 220.6 %shard_map.93 = (bf16[8,512,2048]{2,1,0:T(8,128)(2,1)}, bf16[8,512,2176]{2,1,0:T(8,128)(2,1)}, bf16[2,512,768]{2,1,0:T(8,128)(2,1)}, bf16[2,384,512]{2,1,0:T(8,128)(2,1)}, bf16[128,2176]{1,0:T(8,128)(2,1)}) custom-call(bf16[128,2048]{1,0:T(8,128)(2,1)} %tok.1, bf16[128,2176]{1,0:T(8,128)(2,1)} %pad_maximum_fusion.gaug, bf16[2,2048,768]{2,1,0:T(8,128)(2,1)} %wgu.1, ...), custom_call_target="tpu_custom_call" | custom-call | tf_op jit(solution)/shard_map/pallas_call | solution.py:239
  225.1 0.8 slice_convert_fusion
  225.8 0.4 select_reduce_fusion
  226.2 1.9 slice.6
  228.1 0.7 copy.14
  228.8 0.0 copy-start
  228.8 2.7 %copy.17 = bf16[2,512,768]{2,1,0:T(8,128)(2,1)} copy(bf16[2,512,768]{2,1,0:T(8,128)(2,1)} %get-tuple-element.20) | data formatting | bytes 3145728
  231.5 0.0 copy-done
  231.5 0.9 copy.18
Async XLA Ops:
  228.8 2.7 %copy-start = (bf16[2,384,512]{2,1,0:T(8,128)(2,1)S(1)}, bf16[2,384,512]{2,1,0:T(8,128)(2,1)}, u32[]{:S(2)}) copy-start(bf16[2,384,512]{2,1,0:T(8,128)(2,1)} %get-tuple-element.21) | copy-start | bytes 2359300

commit v2 on v1

--- a/solution.py
+++ b/solution.py
@@ -10,7 +10,7 @@
 PAD = 128
 
 
-def fused_kernel(tok, gaug, wgu, wd, t_all, g_all, o_gu, o_dn, o_tok,
+def fused_kernel(tok, gaug, wgu, wd, t_all, g_all, o_gu, o_dn, o_tok, o_dr,
                  xbuf, gbuf, gp, sh, dr, acc_gu, acc_dn, part, half, last,
                  rt, rg, st, sg, zt, zg, loc, pr, ps, fr, fs):
     rows = tok.shape[0]
@@ -82,14 +82,15 @@
     ff = wd.shape[1]
     count = wgu.shape[0]
 
-    def unit(u):
-        ca = pltpu.make_async_copy(t_all.at[u], xbuf, loc.at[0])
-        cb = pltpu.make_async_copy(g_all.at[u], gbuf, loc.at[1])
+    def unit(u, c, h):
+        own = pl.ds(h * 2 * rows, 2 * rows)
+        ca = pltpu.make_async_copy(t_all.at[u, own], xbuf, loc.at[0])
+        cb = pltpu.make_async_copy(g_all.at[u, own], gbuf, loc.at[1])
         ca.start()
         cb.start()
         ca.wait()
         cb.wait()
-        dr[...] = jnp.zeros_like(dr)
+        dr[c, own] = jnp.zeros((2 * rows, PAD), jnp.float32)
 
         @pl.loop(0, count)
         def _(j):
@@ -105,14 +106,14 @@
             sig = jax.nn.sigmoid(gate)
             act = gate * sig
             hid = (act * up).astype(jnp.bfloat16).astype(jnp.float32)
-            dr[...] += jnp.where(mine, jnp.sum(back * hid, axis=1, keepdims=True), 0.0)
+            dr[c, own] += jnp.where(mine, jnp.sum(back * hid, axis=1, keepdims=True), 0.0)
             sc = wcol * back
-            gp[j, :, :ff] = (sc * up * sig * (1.0 + gate * (1.0 - sig))).astype(jnp.bfloat16)
-            gp[j, :, ff:] = (sc * act).astype(jnp.bfloat16)
+            gp[c, j, own, :ff] = (sc * up * sig * (1.0 + gate * (1.0 - sig))).astype(jnp.bfloat16)
+            gp[c, j, own, ff:] = (sc * act).astype(jnp.bfloat16)
             sh[...] = (wcol * hid).astype(jnp.bfloat16)
             cols = pl.ds(pl.multiple_of(z * width_gu, 128), width_gu)
             cold = pl.ds(pl.multiple_of(z * width_dn, 128), width_dn)
-            acc_gu[j] += lax.dot_general(xbuf[:, cols], gp[j], (((0,), (0,)), ((), ())),
+            acc_gu[j] += lax.dot_general(xbuf[:, cols], gp[c, j, own], (((0,), (0,)), ((), ())),
                                          preferred_element_type=jnp.float32)
             acc_dn[j] += lax.dot_general(sh[...], gbuf[:, cold], (((0,), (0,)), ((), ())),
                                          preferred_element_type=jnp.float32)
@@ -123,13 +124,13 @@
         @pl.loop(0, dm // step)
         def _(n):
             cols = pl.ds(pl.multiple_of(n * step, 128), step)
-            total = lax.dot_general(gp[0], wgu[0, cols, :], (((1,), (1,)), ((), ())),
+            total = lax.dot_general(gp[c, 0], wgu[0, cols, :], (((1,), (1,)), ((), ())),
                                     preferred_element_type=jnp.float32)
             for j in range(1, count):
-                total += lax.dot_general(gp[j], wgu[j, cols, :], (((1,), (1,)), ((), ())),
+                total += lax.dot_general(gp[c, j], wgu[j, cols, :], (((1,), (1,)), ((), ())),
                                          preferred_element_type=jnp.float32)
             part[c, :, cols] = total.astype(jnp.bfloat16)
-        part[c, :, dm:] = dr[...].astype(jnp.bfloat16)
+        part[c, :, dm:] = dr[c].astype(jnp.bfloat16)
 
     to_core = pltpu.make_async_remote_copy(
         src_ref=part.at[1], dst_ref=half, send_sem=ps, recv_sem=pr,
@@ -145,7 +146,7 @@
 
         @pl.when(i > 0)
         def _():
-            unit(2 * i - 1)
+            unit(2 * i - 1, 1, 1)
 
         @pl.when(i == 1)
         def _():
@@ -163,7 +164,7 @@
 
         @pl.when(i > 0)
         def _():
-            unit(2 * i - 2)
+            unit(2 * i - 2, 0, 1)
 
         @pl.when(i == 1)
         def _():
@@ -188,11 +189,16 @@
 
         @pl.when(i < 4)
         def _():
+            unit(u, 0, 0)
+            for k in range(2):
+                got(t_all, rt, u + 1, k)
+                got(g_all, rg, u + 1, k)
+            unit(u + 1, 1, 0)
             got(t_all, rt, u, 3)
             t_c(u, 3).start()
             got(g_all, rg, u, 3)
             g_c(u, 3).start()
-            for k in range(4):
+            for k in (2, 3):
                 got(t_all, rt, u + 1, k)
                 got(g_all, rg, u + 1, k)
 
@@ -203,7 +209,8 @@
     total = part[0, pl.ds(0, rows), :].astype(jnp.float32)
     for k in range(3):
         total += last[k].astype(jnp.float32)
-    o_tok[...] = total.astype(jnp.bfloat16)
+    o_tok[...] = total[:, :dm].astype(jnp.bfloat16)
+    o_dr[...] = total[:, dm:].astype(jnp.bfloat16)
 
     to_core.wait_send()
     for c in to_owner:
@@ -236,23 +243,24 @@
     dma = pltpu.SemaphoreType.DMA
     vm = pl.BlockSpec(memory_space=pltpu.VMEM)
     anyw = pl.BlockSpec(memory_space=pl.ANY)
-    _, _, o_gu, o_dn, o_tok = pl.pallas_call(
+    _, _, o_gu, o_dn, o_tok, o_dr = pl.pallas_call(
         fused_kernel,
         out_shape=(
             jax.ShapeDtypeStruct((units, 4 * rows, dm), bf),
             jax.ShapeDtypeStruct((units, 4 * rows, dm + PAD), bf),
             jax.ShapeDtypeStruct((count, dm // n_dp, width), bf),
             jax.ShapeDtypeStruct((count, ff, dm // n_dp), bf),
-            jax.ShapeDtypeStruct((rows, dm + PAD), bf),
+            jax.ShapeDtypeStruct((rows, dm), bf),
+            jax.ShapeDtypeStruct((rows, PAD), bf),
         ),
         in_specs=[vm] * 4,
-        out_specs=(anyw, anyw, vm, vm, vm),
+        out_specs=(anyw, anyw, vm, vm, vm, vm),
         scratch_shapes=[
-            pltpu.VMEM((4 * rows, dm), bf),
-            pltpu.VMEM((4 * rows, dm + PAD), bf),
-            pltpu.VMEM((count, 4 * rows, width), bf),
-            pltpu.VMEM((4 * rows, ff), bf),
-            pltpu.VMEM((4 * rows, PAD), f32),
+            pltpu.VMEM((2 * rows, dm), bf),
+            pltpu.VMEM((2 * rows, dm + PAD), bf),
+            pltpu.VMEM((2, count, 4 * rows, width), bf),
+            pltpu.VMEM((2 * rows, ff), bf),
+            pltpu.VMEM((2, 4 * rows, PAD), f32),
             pltpu.VMEM((count, dm // n_dp, width), f32),
             pltpu.VMEM((count, ff, dm // n_dp), f32),
             pltpu.VMEM((2, 4 * rows, dm + PAD), bf),
@@ -265,8 +273,8 @@
         compiler_params=pltpu.CompilerParams(
             collective_id=0, has_side_effects=True, vmem_limit_bytes=60 * 1024 * 1024),
     )(tokens, gaug, w_gate_up, w_down)
-    d_route = jnp.sum(jnp.where(onehot, o_tok[:, None, dm:].astype(f32), 0.0), axis=2).astype(bf)
-    return o_tok[:, :dm], d_route, o_gu, o_dn
+    d_route = jnp.sum(jnp.where(onehot, o_dr[:, None, :].astype(f32), 0.0), axis=2).astype(bf)
+    return o_tok, d_route, o_gu, o_dn
 
 
 def expert_backward(rows_in, rows_grad, weight, gate_up, down):

time: 233 us -> 228 us (0.979)
  Pallas kernels: 221 us -> 216 us
    pallas_call x1, Pallas kernels: 221 us -> 216 us  [local_fused(): pl.pallas_call(fused_kernel, out_shape=(jax.ShapeDtypeStruct((units, 4 *...]
    unnamed x6 -> x7, local copies, waits for them, and re-layouts: 5.05 us -> 6.94 us
where the time goes in v2:
time: 228 us; the launch traced here: 227 us
  Pallas kernels  216 us (95%)
  local copies, waits for them, and re-layouts  7.72 us (3%)
  other arithmetic  3.41 us (1%)
    pallas_call x1, Pallas kernels, local_fused(): pl.pallas_call(fused_kernel, out_shape=(jax.ShapeDtypeStruct((units, 4 *...  216 us
    unnamed x7, local copies, waits for them, and re-layouts  6.94 us

profile of v2, /device:TPU:1, one launch (start us, length us, event | category | flops | bytes accessed | tf_op | source)
XLA Modules:
  0.0 227.3 jit_solution(8221569733703133632)
XLA Ops:
  0.6 0.8 copy.12
  1.4 0.8 copy.13
  2.2 0.4 select_reduce_fusion.1
  2.6 1.9 pad_maximum_fusion.gaug
  4.5 215.5 %shard_map.93 = (bf16[8,512,2048]{2,1,0:T(8,128)(2,1)}, bf16[8,512,2176]{2,1,0:T(8,128)(2,1)}, bf16[2,512,768]{2,1,0:T(8,128)(2,1)}, bf16[2,384,512]{2,1,0:T(8,1...) custom-call(bf16[128,2048]{1,0:T(8,128)(2,1)} %tok.1, bf16[128,2176]{1,0:T(8,128)(2,1)} %pad_maximum_fusion.gaug, ...), custom_call_target="tpu_custom_call" | custom-call | tf_op jit(solution)/shard_map/pallas_call | solution.py:246
  220.0 0.8 convert_element_type.16
  220.8 0.4 select_reduce_fusion
  221.2 0.7 copy.14
  221.8 1.9 copy.18
  223.7 0.0 copy-start
  223.7 2.7 %copy.19 = bf16[2,512,768]{2,1,0:T(8,128)(2,1)} copy(bf16[2,512,768]{2,1,0:T(8,128)(2,1)} %get-tuple-element.22) | data formatting | bytes 3145728
  226.4 0.0 copy-done
  226.4 0.9 copy.20
Async XLA Ops:
  223.7 2.7 %copy-start = (bf16[2,384,512]{2,1,0:T(8,128)(2,1)S(1)}, bf16[2,384,512]{2,1,0:T(8,128)(2,1)}, u32[]{:S(2)}) copy-start(bf16[2,384,512]{2,1,0:T(8,128)(2,1)} %get-tuple-element.23) | copy-start | bytes 2359300
